TPU v7x, 512 devices: a whole 4x4x16 slice. The times are simulated.
512 devices in a mesh: seq: 128 (over y, z, core), tp: 4 (over x).
Axes of the slice: x: 4, y: 4, z: 16, core: 2. Of those that a mesh axis runs over, the one named last changes fastest.
Arguments:
- queries: float32 [16384, 2048], P('seq', 'tp'), may hold values from -6 to 6
- keys: float32 [16384, 2048], P('seq', 'tp'), may hold values from -6 to 6
- values: float32 [16384, 2048], P('seq', 'tp'), may hold values from -6 to 6
- out_weight: float32 [2048, 4096], P('seq', 'tp'), may hold values from -0.125 to 0.125
Outputs:
- mixed: float32 [16384, 4096], P('seq', 'tp')
All inputs are finite; a program needn't handle non-finite values.
Results may differ from a plain program's by a relative error of at most 0.0003.
Values sent between devices are 32-bit elements; how exact they have to be, the bound alone decides.
A program may use at most 128 MiB of HBM per device.

v0:
```python
import jax
import jax.numpy as jnp
from jax import lax
from jax.sharding import PartitionSpec as P

DH = 128


def prefix(part, axis, combine, identity):
    place = lax.axis_index(axis)
    gathered = jax.tree.map(lambda a: lax.all_gather(a, axis), part)
    state = jax.tree.map(lambda a, e: jnp.zeros_like(a) + jnp.asarray(e, a.dtype), part, identity)

    def one(step, state):
        return combine(
            state, jax.tree.map(lambda a: lax.dynamic_index_in_dim(a, step, 0, False), gathered)
        )

    return lax.fori_loop(0, place, one, state)


def features(inputs):
    return jnp.where(inputs > 0, inputs + 1.0, jnp.exp(jnp.minimum(inputs, 0.0)))


def combine(earlier, later):
    return (earlier[0] + later[0], earlier[1] + later[1])


def shards(queries, keys, values, out_weight):
    highest = lax.Precision.HIGHEST
    tok_rows = queries.shape[0]
    heads_here = queries.shape[1] // DH
    phi_queries = features(queries).reshape(tok_rows, heads_here, DH)
    phi_keys = features(keys).reshape(tok_rows, heads_here, DH)
    value_heads = values.reshape(tok_rows, heads_here, DH)
    memory_state = jnp.einsum("shd,she->hde", phi_keys, value_heads, precision=highest)
    key_total = jnp.sum(phi_keys, axis=0)
    identity = (jnp.zeros_like(memory_state), jnp.zeros_like(key_total))
    prior_state, prior_total = prefix((memory_state, key_total), "seq", combine, identity)
    causal_mask = jnp.arange(tok_rows)[:, None] >= jnp.arange(tok_rows)[None, :]
    scores = jnp.einsum("thd,shd->hts", phi_queries, phi_keys, precision=highest)
    scores = jnp.where(causal_mask[None], scores, 0.0)
    numerator = jnp.einsum("hts,shd->thd", scores, value_heads, precision=highest)
    numerator = numerator + jnp.einsum("thd,hde->the", phi_queries, prior_state, precision=highest)
    denominator = jnp.sum(scores, axis=2).T + jnp.einsum(
        "thd,hd->th", phi_queries, prior_total, precision=highest
    )
    attended = (numerator / denominator[:, :, None]).reshape(tok_rows, heads_here * DH)
    every_head = lax.all_gather(attended, "tp", axis=1, tiled=True)
    gathered = lax.all_gather(out_weight, "seq", axis=0, tiled=True)
    mixed = jnp.dot(every_head, gathered, precision=highest, preferred_element_type=jnp.float32)
    return mixed


def solution(mesh):
    return jax.shard_map(
        shards,
        mesh=mesh,
        in_specs=(P("seq", "tp"), P("seq", "tp"), P("seq", "tp"), P("seq", "tp")),
        out_specs=P("seq", "tp"),
        check_vma=False,
    )
```

profile of v0, /device:TPU:1, one launch (start us, length us, event | category | flops | bytes accessed | tf_op | source)
XLA Modules:
  0.0 401.2 jit_solution(6245858117362999715)
XLA Ops:
  6.5 0.0 copy-start
  6.5 0.0 all-gather.9.cloned.1.call-start
  6.5 1.1 fusion.7
  7.6 0.1 copy.31
  7.7 0.0 copy-done
  7.8 1.1 fusion.3
  8.8 0.0 all-gather.9.cloned.1.call-update
  8.9 0.0 all-gather.7.cloned.1.call-start
  8.9 0.7 all-gather.7.cloned.1.call-update
  9.6 0.0 all-gather.5.cloned.1.call-start
  9.7 1.0 exponential_select_fusion.1
  10.7 0.1 copy.30
  10.8 108.5 %all_gather.21 = f32[128,4,128]{2,1,0:T(4,128)S(1)} all-gather(f32[1,4,128]{2,1,0:T(4,128)S(1)} %bitcast.58), channel_id=1, replica_groups=mesh['seq'=128,'tp'=4] {'seq'}, dimensions={0}, use_global_device_ids=true | all-gather | bytes 264192 | tf_op jit(solution)/shard_map/all_gather | solution.py:11
  119.4 0.6 fusion.8
  120.0 0.6 convolution_bitcast_fusion.1
  120.6 90.9 %all-gather.9.cloned.1.call-done = f32[512,128,128]{2,1,0:T(8,128)} async-done(((f32[4,128,128]{2,1,0:T(8,128)}), f32[512,128,128]{2,1,0:T(8,128)}) %all-gather.9.cloned.1.call-update) | async-done | bytes 33554448 | tf_op jit(solution)/shard_map/all_gather | solution.py:11
  211.6 1.1 while.12
  211.6 1.0 bitcast_add_fusion.4
  212.6 0.3 fusion.9
  212.9 1.3 fusion.1
  214.3 0.0 all-gather.5.cloned.1.call-update
  214.3 143.7 %all-gather.7.cloned.1.call-done = f32[2048,1024]{1,0:T(8,128)} async-done(((f32[16,1024]{1,0:T(8,128)}), f32[2048,1024]{1,0:T(8,128)}) %all-gather.7.cloned.1.call-update) | async-done | bytes 8388624 | tf_op jit(solution)/shard_map/all_gather | solution.py:51
  358.0 27.5 %all-gather.5.cloned.1.call-done = f32[128,2048]{0,1:T(8,128)} async-done(((f32[128,512]{0,1:T(8,128)}), f32[128,2048]{0,1:T(8,128)}) %all-gather.5.cloned.1.call-update) | async-done | bytes 1048592 | tf_op jit(solution)/shard_map/all_gather | solution.py:50
  385.5 9.1 %fusion.10 = f32[128,1024]{1,0:T(8,128)} fusion(f32[128,2048]{0,1:T(8,128)} %all-gather.5.cloned.1.call-done, f32[2048,1024]{1,0:T(8,128)} %all-gather.7.cloned.1.call-done), kind=kOutput, calls=%fused_computation.19 | convolution fusion | flops 3221225472 | bytes 9961472 | tf_op jit(solution)/shard_map/dot_general | solution.py:52
  (5 shorter events, 0.1 us)
Async XLA Ops:
  6.5 1.2 copy-start
  6.5 205.0 %all-gather.9.cloned.1.call-start = ((), (), s32[]{:S(2)}) async-start(), calls=%async_computation.2 | async-start | bytes 33816576 | tf_op jit(solution)/shard_map/all_gather | solution.py:11
  8.9 349.1 %all-gather.7.cloned.1.call-start = ((), (), s32[]{:S(2)}) async-start(), calls=%async_computation.1 | async-start | bytes 8454144 | tf_op jit(solution)/shard_map/all_gather | solution.py:51
  9.6 375.9 %all-gather.5.cloned.1.call-start = ((), (), s32[]{:S(2)}) async-start(), calls=%async_computation | async-start | bytes 1310720 | tf_op jit(solution)/shard_map/all_gather | solution.py:50
Sparse Core Ops, SparseCore 0:
  10.5 200.9 all-gather.8
  214.7 143.2 all-gather.6
  360.1 25.3 all-gather.4
where the time goes:
time: 405 us; the launch traced here: 401 us
  waiting for transfers between devices  263 us (65%)
  blocking collectives  109 us (27%)
  between operations  13.2 us (3%)
  matrix products  13.1 us (3%)
    all_gather x1, waiting for transfers between devices, shards(): gathered = lax.all_gather(out_weight, 'seq', axis=0, tiled=True)  144 us
    all_gather x1, blocking collectives, prefix(): gathered = jax.tree.map(lambda a: lax.all_gather(a, axis), part)  109 us
    all_gather x1, waiting for transfers between devices, prefix(): gathered = jax.tree.map(lambda a: lax.all_gather(a, axis), part)  90.9 us
    all_gather x1, waiting for transfers between devices, shards(): every_head = lax.all_gather(attended, 'tp', axis=1, tiled=True)  27.5 us
    dot_general x1, matrix products, shards(): jnp.dot(every_head, gathered, precision=highest, preferred_element_type=j...  9.14 us
  transfers between devices with their start and end apart: 3, of which 3 were waited for; matrix products, arithmetic and copies ran while one was open for 1% of the time, Pallas kernels for 0%

commit v1 on v0

v1 whole, which is shorter than its diff:
```python
import functools

import jax
import jax.numpy as jnp
from jax import lax
from jax.experimental import pallas as pl
from jax.experimental.pallas import tpu as pltpu
from jax.sharding import PartitionSpec as P

MESH = pl.DeviceIdType.MESH
F32 = jnp.float32
BF16 = jnp.bfloat16
HIGHEST = lax.Precision.HIGHEST
DH = 128
NY = 4
TILE = 256


def phi(a):
    return jnp.where(a > 0, a + 1.0, jnp.exp(jnp.minimum(a, 0.0)))


def rc(src, dst, send_sem, recv_sem, dev):
    return pltpu.make_async_remote_copy(
        src_ref=src, dst_ref=dst, send_sem=send_sem, recv_sem=recv_sem,
        device_id=dev, device_id_type=MESH,
    )


def halves(a):
    high = a.astype(BF16)
    return high, (a - high.astype(F32)).astype(BF16)


def kernel(
    nz, nx, q_ref, k_ref, v_ref, w_ref, out_ref,
    w_all, st, sx, ps, r1, yt, yr, s2, r2, fs, full, phiq, numl, denl, att, acat,
    zr_s, zr_r, zl_s, zl_r, yp_s, yp_r, ym_s, ym_r, fd_s, fd_r, sb_s, sb_r,
    e_s, e_r, p1_s, p1_r, yx_s, yx_r, p2_s, p2_r,
    xr_s, xr_r, xl_s, xl_r, gr_s, gr_r, gl_s, gl_r,
):
    s, x = lax.axis_index("seq"), lax.axis_index("tp")
    c = lax.rem(s, 2)
    z = lax.rem(s // 2, nz)
    y = s // (2 * nz)
    tok = q_ref.shape[0]
    rows = 2 * DH // nz

    def at(yy, zz, cc):
        return {"seq": (yy * nz + zz) * 2 + cc}

    def dz(k):
        return lax.rem(z + (k + nz), nz)

    def dy(k):
        return lax.rem(y + (k + NY), NY)

    sib = at(y, z, 1 - c)
    right, left = {"tp": lax.rem(x + 1, nx)}, {"tp": lax.rem(x + nx - 1, nx)}

    barrier = pltpu.get_barrier_semaphore()
    pl.semaphore_signal(barrier, inc=1, device_id=sib, device_id_type=MESH)
    for dev in (right, left):
        pl.semaphore_signal(barrier, inc=1, device_id=dev, device_id_type=MESH)
    for k in range(1, NY):
        pl.semaphore_signal(barrier, inc=1, device_id=at(dy(k), z, c), device_id_type=MESH)
    for k in range(1, nz):
        pl.semaphore_signal(barrier, inc=1, device_id=at(y, dz(k), c), device_id_type=MESH)

    row8 = lax.broadcasted_iota(jnp.int32, (8, DH), 0)
    per = nz // 2
    for b in range(2):
        totals = jnp.zeros((8, DH), F32)
        for hh in range(2):
            h = 2 * b + hh
            cols = slice(h * DH, (h + 1) * DH)
            pk = phi(k_ref[:, cols])
            state = lax.dot_general(
                pk, v_ref[:, cols], (((0,), (0,)), ((), ())),
                precision=HIGHEST, preferred_element_type=F32,
            )
            st[b, hh * per:(hh + 1) * per, 0:rows, :] = state.reshape(per, rows, DH)
            total = jnp.sum(pk, axis=0, keepdims=True)
            totals = jnp.where(row8 == hh, jnp.broadcast_to(total, (8, DH)), totals)
        st[b, :, rows:rows + 8, :] = jnp.broadcast_to(totals[None], (nz, 8, DH))
    w_all[y, z, c] = w_ref[...]
    yr[y] = jnp.zeros((rows + 8, DH), F32)

    pl.semaphore_wait(barrier, 1 + 2 + (NY - 1) + (nz - 1))

    sends = []

    def go(copy):
        copy.start()
        sends.append(copy)

    half = nz // 2

    def zof(m):
        return z if m == 0 else (dz(-m) if m <= half else dz(m - half))

    def slot(yy, m, cc):
        return w_all.at[yy, zof(m), cc]

    def to_sib(k, m):
        ref = slot(dy(-k), m, c)
        go(rc(ref, ref, sb_s.at[k, m], sb_r.at[k, m], sib))

    def have(m):
        src = w_ref if m == 0 else slot(y, m, c)
        dst = slot(y, m, c)
        go(rc(src, dst, yp_s.at[m], yp_r.at[m], at(dy(1), z, c)))
        go(rc(src, dst, ym_s.at[m], ym_r.at[m], at(dy(-1), z, c)))
        go(rc(src, dst, sb_s.at[0, m], sb_r.at[0, m], sib))

    def z_round(r):
        if r == 0:
            dst = slot(y, 0, c)
            go(rc(w_ref, dst, zr_s.at[0], zr_r.at[0], at(y, dz(1), c)))
            go(rc(w_ref, dst, zl_s.at[0], zl_r.at[0], at(y, dz(-1), c)))
            have(0)
            return
        ref = slot(y, r, c)
        rc(ref, ref, zr_s.at[r - 1], zr_r.at[r - 1], at(y, dz(1), c)).wait_recv()
        if r < half:
            go(rc(ref, ref, zr_s.at[r], zr_r.at[r], at(y, dz(1), c)))
        if r < half:
            ref = slot(y, half + r, c)
            rc(ref, ref, zl_s.at[r - 1], zl_r.at[r - 1], at(y, dz(-1), c)).wait_recv()
            if r < half - 1:
                go(rc(ref, ref, zl_s.at[r], zl_r.at[r], at(y, dz(-1), c)))
        have(r)
        if r < half:
            have(half + r)

    def y_stage(r):
        for m in ((r,) if r in (0, half) else (r, half + r)):
            below, above = slot(dy(-1), m, c), slot(dy(1), m, c)
            rc(below, below, yp_s.at[m], yp_r.at[m], at(dy(1), z, c)).wait_recv()
            if m < half:
                go(rc(below, below, fd_s.at[m], fd_r.at[m], at(dy(1), z, c)))
            to_sib(1, m)
            rc(above, above, ym_s.at[m], ym_r.at[m], at(dy(-1), z, c)).wait_recv()
            if m >= half:
                go(rc(above, above, fd_s.at[m], fd_r.at[m], at(dy(-1), z, c)))
            to_sib(3, m)

    def far_stage(m):
        ref = slot(dy(2), m, c)
        rc(ref, ref, fd_s.at[m], fd_r.at[m], at(dy(1), z, c)).wait_recv()
        to_sib(2, m)

    go(rc(st.at[1 - c], sx, e_s.at[0], e_r.at[0], sib))
    z_round(0)
    rc(st.at[1 - c], sx, e_s.at[0], e_r.at[0], sib).wait_recv()
    ps[...] = st[c] + sx[...]

    def send1(k, carry):
        peer = lax.rem(z + k, nz)
        rc(ps.at[peer], r1.at[z], p1_s.at[k], p1_r.at[k], at(y, peer, c)).start()
        return carry

    lax.fori_loop(1, nz, send1, 0)
    r1[z] = ps[z]

    causal = lax.broadcasted_iota(jnp.int32, (tok, tok), 0) >= lax.broadcasted_iota(
        jnp.int32, (tok, tok), 1
    )
    for h in range(4):
        cols = slice(h * DH, (h + 1) * DH)
        pq, pk = phi(q_ref[:, cols]), phi(k_ref[:, cols])
        scores = lax.dot_general(
            pq, pk, (((1,), (1,)), ((), ())), precision=HIGHEST, preferred_element_type=F32
        )
        scores = jnp.where(causal, scores, 0.0)
        phiq[h] = pq
        numl[h] = jnp.dot(
            scores, v_ref[:, cols], precision=HIGHEST, preferred_element_type=F32
        )
        denl[h] = jnp.broadcast_to(jnp.sum(scores, axis=1, keepdims=True), (tok, DH))

    z_round(1)
    z_round(2)

    def wait1(k, carry):
        origin = lax.rem(z + nz - k, nz)
        rc(ps.at[0], r1.at[origin], p1_s.at[k], p1_r.at[k], at(y, origin, c)).wait_recv()
        return carry

    lax.fori_loop(1, nz, wait1, 0)
    acc = jnp.zeros((rows + 8, DH), F32)
    for i in range(nz):
        s2[i] = acc
        acc = acc + r1[i]
    yt[...] = acc
    for k in range(1, NY):
        go(rc(yt, yr.at[y], yx_s.at[k], yx_r.at[k], at(dy(k), z, c)))
    z_round(3)
    y_stage(0)
    for k in range(1, NY):
        rc(yt, yr.at[dy(-k)], yx_s.at[k], yx_r.at[k], at(dy(k), z, c)).wait_recv()
    base = jnp.zeros((rows + 8, DH), F32)
    for yy in range(NY):
        base = base + jnp.where(yy < y, yr[yy], 0.0)
    for i in range(nz):
        s2[i] = s2[i] + base

    def send2(k, carry):
        peer = lax.rem(z + k, nz)
        rc(
            s2.at[peer, pl.ds(0, rows)], r2.at[z, pl.ds(0, rows)],
            p2_s.at[k], p2_r.at[k], at(y, peer, c),
        ).start()
        return carry

    lax.fori_loop(1, nz, send2, 0)
    r2[z, 0:rows, :] = s2[z, 0:rows, :]
    r2[:, rows:rows + 8, :] = jnp.broadcast_to(s2[z, rows:rows + 8, :][None], (nz, 8, DH))

    z_round(4)
    y_stage(1)
    z_round(5)
    y_stage(2)
    z_round(6)
    y_stage(3)

    def wait2(k, carry):
        origin = lax.rem(z + nz - k, nz)
        rc(
            s2.at[0, pl.ds(0, rows)], r2.at[origin, pl.ds(0, rows)],
            p2_s.at[k], p2_r.at[k], at(y, origin, c),
        ).wait_recv()
        return carry

    lax.fori_loop(1, nz, wait2, 0)
    fs[...] = r2[...] + jnp.where(c == 0, st[c], 0.0)
    go(rc(fs, full.at[c], e_s.at[1], e_r.at[1], sib))
    full[c] = r2[...] + jnp.where(c == 1, sx[...], 0.0)

    for t in range(4):
        h, hh = lax.rem(2 * c + t, 4), t % 2
        b = c if t < 2 else 1 - c
        if t == 2:
            rc(fs, full.at[1 - c], e_s.at[1], e_r.at[1], sib).wait_recv()
        prior = full[b, hh * per:(hh + 1) * per, 0:rows, :].reshape(DH, DH)
        total = full[b, 0, rows + hh:rows + hh + 1, :]
        pq = phiq[h]
        num = numl[h] + jnp.dot(pq, prior, precision=HIGHEST, preferred_element_type=F32)
        den = denl[h] + jnp.sum(pq * total, axis=1, keepdims=True)
        att[x, h] = num / den
        go(rc(att.at[x, h], att.at[x, h], xr_s.at[t], xr_r.at[t], right))
        go(rc(att.at[x, h], att.at[x, h], xl_s.at[t], xl_r.at[t], left))

    z_round(7)
    y_stage(4)
    z_round(8)

    xl, xr, xf = lax.rem(x + nx - 1, nx), lax.rem(x + 1, nx), lax.rem(x + 2, nx)
    for t in range(4):
        h = lax.rem(2 * c + t, 4)
        ref = att.at[xl, h]
        rc(ref, ref, xr_s.at[t], xr_r.at[t], right).wait_recv()
        if t % 2 == 0:
            go(rc(ref, ref, gr_s.at[t], gr_r.at[t], right))
        ref = att.at[xr, h]
        rc(ref, ref, xl_s.at[t], xl_r.at[t], left).wait_recv()
        if t % 2 == 1:
            go(rc(ref, ref, gl_s.at[t], gl_r.at[t], left))

    for r in range(5, half + 1):
        y_stage(r)
    for m in range(nz):
        far_stage(m)
    for t in range(4):
        h = lax.rem(2 * c + t, 4)
        ref = att.at[xf, h]
        if t % 2 == 0:
            rc(ref, ref, gr_s.at[t], gr_r.at[t], right).wait_recv()
        else:
            rc(ref, ref, gl_s.at[t], gl_r.at[t], left).wait_recv()
    for k in range(NY):
        for m in range(nz):
            ref = slot(dy(-k), m, 1 - c)
            rc(ref, ref, sb_s.at[k, m], sb_r.at[k, m], sib).wait_recv()

    for xx in range(nx):
        for h in range(4):
            high, low = halves(att[xx, h])
            acat[xx, 0:tok, h * DH:(h + 1) * DH] = high
            acat[xx, tok:2 * tok, h * DH:(h + 1) * DH] = low

    def tile(n, carry):
        cols = pl.ds(pl.multiple_of(n * TILE, TILE), TILE)
        total = jnp.zeros((tok, TILE), F32)
        for xx in range(nx):
            wt = w_all[xx, :, :, :, cols].reshape(4 * DH, TILE)
            high, low = halves(wt)
            both = jnp.dot(acat[xx], high, preferred_element_type=F32)
            total = total + (
                both[0:tok] + both[tok:2 * tok]
                + jnp.dot(acat[xx, 0:tok, :], low, preferred_element_type=F32)
            )
        out_ref[:, cols] = total
        return carry

    lax.fori_loop(0, out_ref.shape[1] // TILE, tile, 0)

    for copy in sends:
        copy.wait_send()

    def sent(k, carry):
        peer = lax.rem(z + k, nz)
        rc(ps.at[peer], r1.at[z], p1_s.at[k], p1_r.at[k], at(y, peer, c)).wait_send()
        rc(
            s2.at[peer, pl.ds(0, rows)], r2.at[z, pl.ds(0, rows)],
            p2_s.at[k], p2_r.at[k], at(y, peer, c),
        ).wait_send()
        return carry

    lax.fori_loop(1, nz, sent, 0)


def solution(mesh):
    nz, nx = mesh.shape["seq"] // (2 * NY), mesh.shape["tp"]

    def shards(queries, keys, values, out_weight):
        tok = queries.shape[0]
        depth, columns = out_weight.shape
        part = (nz, 2 * DH // nz + 8, DH)
        dma = pltpu.SemaphoreType.DMA
        vmem = pl.BlockSpec(memory_space=pltpu.VMEM)
        return pl.pallas_call(
            functools.partial(kernel, nz, nx),
            out_shape=jax.ShapeDtypeStruct((tok, columns), F32),
            in_specs=[vmem] * 4,
            out_specs=vmem,
            scratch_shapes=[
                pltpu.VMEM((NY, nz, 2, depth, columns), F32),
                pltpu.VMEM((2,) + part, F32),
                pltpu.VMEM(part, F32),
                pltpu.VMEM(part, F32),
                pltpu.VMEM(part, F32),
                pltpu.VMEM(part[1:], F32),
                pltpu.VMEM((NY,) + part[1:], F32),
                pltpu.VMEM(part, F32),
                pltpu.VMEM(part, F32),
                pltpu.VMEM(part, F32),
                pltpu.VMEM((2,) + part, F32),
                pltpu.VMEM((4, tok, DH), F32),
                pltpu.VMEM((4, tok, DH), F32),
                pltpu.VMEM((4, tok, DH), F32),
                pltpu.VMEM((nx, 4, tok, DH), F32),
                pltpu.VMEM((nx, 2 * tok, 4 * DH), BF16),
            ]
            + [dma((nz // 2,))] * 4
            + [dma((nz,))] * 6
            + [dma((NY, nz))] * 2
            + [dma((2,))] * 2
            + [dma((nz,))] * 2
            + [dma((NY,))] * 2
            + [dma((nz,))] * 2
            + [dma((4,))] * 8,
            compiler_params=pltpu.CompilerParams(
                collective_id=0, has_side_effects=True, vmem_limit_bytes=48 << 20
            ),
        )(queries, keys, values, out_weight)

    return jax.shard_map(
        shards,
        mesh=mesh,
        in_specs=(P("seq", "tp"),) * 4,
        out_specs=P("seq", "tp"),
        check_vma=False,
    )
```

time: 405 us -> 77.4 us (0.19)
  waiting for transfers between devices: 263 us -> 0 us
  blocking collectives: 109 us -> 0 us
  Pallas kernels: 0 us -> 72.6 us
  between operations: 13.2 us -> 0.01 us
  matrix products: 13.1 us -> 0 us
  local copies, waits for them, and re-layouts: 0.27 us -> 4.48 us
    all_gather x3 -> x0, waiting for transfers between devices: 262 us -> none  [the longest x1 144 us: shards(): gathered = lax.all_gather(out_weight, 'seq', axis=0, tiled=True)]
    all_gather x1 -> x0, blocking collectives: 109 us -> none  [prefix(): gathered = jax.tree.map(lambda a: lax.all_gather(a, axis), part)]
    pallas_call x0 -> x1, Pallas kernels: none -> 72.6 us  [shards(): pl.pallas_call(functools.partial(kernel, nz, nx), out_shape=jax.ShapeDtyp...]
    dot_general x6 -> x0, matrix products: 13.1 us -> none  [the longest x1 9.14 us: shards(): jnp.dot(every_head, gathered, precision=highest, preferred_element_type=j...]
    unnamed x2 -> x9, local copies, waits for them, and re-layouts: 0.01 us -> 4.48 us
  transfers between devices with their start and end apart: 3 -> 0, of which waited for: 3 -> 0; matrix products, arithmetic and copies ran while one was open for 1% -> 0% of each run, Pallas kernels for 0% -> 0%
where the time goes in v1:
time: 77.4 us; the launch traced here: 77.1 us
  Pallas kernels  72.6 us (94%)
  local copies, waits for them, and re-layouts  4.48 us (6%)
    pallas_call x1, Pallas kernels, shards(): pl.pallas_call(functools.partial(kernel, nz, nx), out_shape=jax.ShapeDtyp...  72.6 us
    unnamed x9, local copies, waits for them, and re-layouts  4.48 us

profile of v1, /device:TPU:1, one launch (start us, length us, event | category | flops | bytes accessed | tf_op | source)
XLA Modules:
  0.0 77.1 jit_solution(4350697174326811184)
XLA Ops:
  0.0 0.0 copy-start
  0.0 0.9 %copy-done = f32[128,512]{1,0:T(8,128)S(1)} copy-done((f32[128,512]{1,0:T(8,128)S(1)}, f32[128,512]{1,0:T(8,128)}, u32[]{:S(2)}) %copy-start) | copy-done | bytes 262168
  1.0 0.0 copy-start.1
  1.0 0.9 %copy-done.1 = f32[128,512]{1,0:T(8,128)S(1)} copy-done((f32[128,512]{1,0:T(8,128)S(1)}, f32[128,512]{1,0:T(8,128)}, u32[]{:S(2)}) %copy-start.1) | copy-done | bytes 262168
  1.9 0.0 copy-start.2
  1.9 0.9 %copy-done.2 = f32[128,512]{1,0:T(8,128)S(1)} copy-done((f32[128,512]{1,0:T(8,128)S(1)}, f32[128,512]{1,0:T(8,128)}, u32[]{:S(2)}) %copy-start.2) | copy-done | bytes 262168
  2.9 0.0 copy-start.3
  2.9 0.8 %copy-done.3 = f32[16,1024]{1,0:T(8,128)S(1)} copy-done((f32[16,1024]{1,0:T(8,128)S(1)}, f32[16,1024]{1,0:T(8,128)}, u32[]{:S(2)}) %copy-start.3) | copy-done | bytes 65560
  3.7 72.6 %shard_map.46 = f32[128,1024]{1,0:T(8,128)S(1)} custom-call(f32[128,512]{1,0:T(8,128)S(1)} %copy-done, f32[128,512]{1,0:T(8,128)S(1)} %copy-done.1, f32[128,512]{1,0:T(8,128)S(1)} %copy-done.2, f32[16,1024]{1,0:T(8,128)S(1)} %copy-done.3), custom_call_target="tpu_custom_call" | custom-call | tf_op jit(solution)/shard_map/pallas_call | solution.py:332
  76.3 0.8 %copy.6 = f32[128,1024]{1,0:T(8,128)} copy(f32[128,1024]{1,0:T(8,128)S(1)} %shard_map.46) | data formatting | bytes 1048576
Async XLA Ops:
  0.0 0.9 %copy-start = (f32[128,512]{1,0:T(8,128)S(1)}, f32[128,512]{1,0:T(8,128)}, u32[]{:S(2)}) copy-start(f32[128,512]{1,0:T(8,128)} %q_ref.1) | copy-start | bytes 786436
  1.0 0.9 %copy-start.1 = (f32[128,512]{1,0:T(8,128)S(1)}, f32[128,512]{1,0:T(8,128)}, u32[]{:S(2)}) copy-start(f32[128,512]{1,0:T(8,128)} %k_ref.1) | copy-start | bytes 786436
  1.9 0.9 %copy-start.2 = (f32[128,512]{1,0:T(8,128)S(1)}, f32[128,512]{1,0:T(8,128)}, u32[]{:S(2)}) copy-start(f32[128,512]{1,0:T(8,128)} %v_ref.1) | copy-start | bytes 786436
  2.9 0.8 %copy-start.3 = (f32[16,1024]{1,0:T(8,128)S(1)}, f32[16,1024]{1,0:T(8,128)}, u32[]{:S(2)}) copy-start(f32[16,1024]{1,0:T(8,128)} %w_ref.1) | copy-start | bytes 196612

commit v2 on v1

v2 whole, which is shorter than its diff:
```python
import functools

import jax
import jax.numpy as jnp
from jax import lax
from jax.experimental import pallas as pl
from jax.experimental.pallas import tpu as pltpu
from jax.sharding import PartitionSpec as P

MESH = pl.DeviceIdType.MESH
F32 = jnp.float32
BF16 = jnp.bfloat16
DH = 128
NY = 4
TILE = 256


def phi(a):
    return jnp.where(a > 0, a + 1.0, jnp.exp(jnp.minimum(a, 0.0)))


def rc(src, dst, send_sem, recv_sem, dev):
    return pltpu.make_async_remote_copy(
        src_ref=src, dst_ref=dst, send_sem=send_sem, recv_sem=recv_sem,
        device_id=dev, device_id_type=MESH,
    )


def halves(a):
    high = a.astype(BF16)
    return high, (a - high.astype(F32)).astype(BF16)


def dot3(a, b, dims):
    (ah, al), (bh, bl) = a, b

    def one(p, r):
        return lax.dot_general(p, r, (dims, ((), ())), preferred_element_type=F32)

    return one(ah, bh) + (one(al, bh) + one(ah, bl))


def kernel(
    nz, nx, q_hbm, k_hbm, v_hbm, w_hbm, out_ref,
    w_all, q_ref, k_ref, v_ref, st, tst, sx, tsx, ps, pt, r1, rt1, yt, yr, s2, r2, fs, full,
    ft, ftot, phiq, qh, ql, numl, denl, att, acat,
    in_s, tok_r, tok_l,
    zr_s, zr_r, zl_s, zl_r, yp_s, yp_r, ym_s, ym_r, fd_s, fd_r, sb_s, sb_r,
    e_s, e_r, p1_s, p1_r, pt_s, pt_r, yx_s, yx_r, p2_s, p2_r,
    xr_s, xr_r, xl_s, xl_r, gr_s, gr_r, gl_s, gl_r,
):
    s, x = lax.axis_index("seq"), lax.axis_index("tp")
    c = lax.rem(s, 2)
    z = lax.rem(s // 2, nz)
    y = s // (2 * nz)
    tok = q_ref.shape[0]
    rows = 2 * DH // nz

    def at(yy, zz, cc):
        return {"seq": (yy * nz + zz) * 2 + cc}

    def dz(k):
        return lax.rem(z + (k + nz), nz)

    def dy(k):
        return lax.rem(y + (k + NY), NY)

    sib = at(y, z, 1 - c)
    right, left = {"tp": lax.rem(x + 1, nx)}, {"tp": lax.rem(x + nx - 1, nx)}
    up, down = at(y, dz(1), c), at(y, dz(-1), c)
    half = nz // 2

    barrier = pltpu.get_barrier_semaphore()
    near = [sib, right, left, up, down] + [at(dy(k), z, c) for k in range(1, NY)]
    for dev in near:
        pl.semaphore_signal(barrier, inc=1, device_id=dev, device_id_type=MESH)
    inputs = [
        pltpu.make_async_copy(src, dst, in_s.at[i])
        for i, (src, dst) in enumerate(
            ((w_hbm, w_all.at[y, z, c]), (k_hbm, k_ref), (v_hbm, v_ref), (q_hbm, q_ref))
        )
    ]
    for copy in inputs:
        copy.start()
    pl.semaphore_wait(barrier, len(near))

    def token(r):
        if r > 1:
            pl.semaphore_wait(tok_l.at[r], 1)
        if r < half:
            pl.semaphore_signal(tok_l.at[r + 1], inc=1, device_id=down, device_id_type=MESH)
        if r < half:
            if r > 1:
                pl.semaphore_wait(tok_r.at[r], 1)
            if r < half - 1:
                pl.semaphore_signal(tok_r.at[r + 1], inc=1, device_id=up, device_id_type=MESH)

    sends = []

    def go(copy):
        copy.start()
        sends.append(copy)

    def zof(m):
        return z if m == 0 else (dz(-m) if m <= half else dz(m - half))

    def slot(yy, m, cc):
        return w_all.at[yy, zof(m), cc]

    def to_sib(k, m):
        ref = slot(dy(-k), m, c)
        go(rc(ref, ref, sb_s.at[k, m], sb_r.at[k, m], sib))

    def have(m):
        src = dst = slot(y, m, c)
        go(rc(src, dst, yp_s.at[m], yp_r.at[m], at(dy(1), z, c)))
        go(rc(src, dst, ym_s.at[m], ym_r.at[m], at(dy(-1), z, c)))
        go(rc(src, dst, sb_s.at[0, m], sb_r.at[0, m], sib))

    def z_round(r):
        if r == 0:
            dst = slot(y, 0, c)
            go(rc(dst, dst, zr_s.at[0], zr_r.at[0], at(y, dz(1), c)))
            go(rc(dst, dst, zl_s.at[0], zl_r.at[0], at(y, dz(-1), c)))
            have(0)
            return
        ref = slot(y, r, c)
        rc(ref, ref, zr_s.at[r - 1], zr_r.at[r - 1], at(y, dz(1), c)).wait_recv()
        if r < half:
            go(rc(ref, ref, zr_s.at[r], zr_r.at[r], at(y, dz(1), c)))
        if r < half:
            ref = slot(y, half + r, c)
            rc(ref, ref, zl_s.at[r - 1], zl_r.at[r - 1], at(y, dz(-1), c)).wait_recv()
            if r < half - 1:
                go(rc(ref, ref, zl_s.at[r], zl_r.at[r], at(y, dz(-1), c)))
        have(r)
        if r < half:
            have(half + r)

    def y_stage(r):
        for m in ((r,) if r in (0, half) else (r, half + r)):
            below, above = slot(dy(-1), m, c), slot(dy(1), m, c)
            rc(below, below, yp_s.at[m], yp_r.at[m], at(dy(1), z, c)).wait_recv()
            if m < half:
                go(rc(below, below, fd_s.at[m], fd_r.at[m], at(dy(1), z, c)))
            to_sib(1, m)
            rc(above, above, ym_s.at[m], ym_r.at[m], at(dy(-1), z, c)).wait_recv()
            if m >= half:
                go(rc(above, above, fd_s.at[m], fd_r.at[m], at(dy(-1), z, c)))
            to_sib(3, m)

    def far_stage(m):
        ref = slot(dy(2), m, c)
        rc(ref, ref, fd_s.at[m], fd_r.at[m], at(dy(1), z, c)).wait_recv()
        to_sib(2, m)

    token(1)
    inputs[0].wait()
    z_round(0)
    inputs[1].wait()
    inputs[2].wait()
    row8 = lax.broadcasted_iota(jnp.int32, (8, DH), 0)
    per = nz // 2
    hops = ((2, 3), (4, 5), (6,), (7, 8))
    for t in range(4):
        b, hh = (1 - c if t < 2 else c), t % 2
        cols = pl.ds(pl.multiple_of((2 * b + hh) * DH, DH), DH)
        pk = phi(k_ref[:, cols])
        state = dot3(halves(pk), halves(v_ref[:, cols]), ((0,), (0,)))
        st[b, hh * per:(hh + 1) * per] = state.reshape(per, rows, DH)
        total = jnp.broadcast_to(jnp.sum(pk, axis=0, keepdims=True), (8, DH))
        if hh == 0:
            totals = total
        else:
            tst[b] = jnp.where(row8 == 0, totals, total)
        if t == 1:
            go(rc(st.at[b], sx, e_s.at[0], e_r.at[0], sib))
            go(rc(tst.at[b], tsx, e_s.at[1], e_r.at[1], sib))
        for r in hops[t]:
            token(r)
        if t == 2:
            z_round(1)
    rc(st.at[1 - c], sx, e_s.at[0], e_r.at[0], sib).wait_recv()
    rc(tst.at[1 - c], tsx, e_s.at[1], e_r.at[1], sib).wait_recv()
    ps[...] = st[c] + sx[...]
    pt[...] = tst[c, 0:2] + tsx[0:2]

    def send1(k, carry):
        peer = lax.rem(z + k, nz)
        rc(ps.at[peer], r1.at[z], p1_s.at[k], p1_r.at[k], at(y, peer, c)).start()
        rc(pt, rt1.at[z], pt_s.at[k], pt_r.at[k], at(y, peer, c)).start()
        return carry

    lax.fori_loop(1, nz, send1, 0)
    r1[z] = ps[z]
    rt1[z] = pt[...]
    yr[y] = jnp.zeros((rows + 8, DH), F32)
    z_round(2)

    inputs[3].wait()
    causal = lax.broadcasted_iota(jnp.int32, (tok, tok), 0) >= lax.broadcasted_iota(
        jnp.int32, (tok, tok), 1
    )
    for h in range(4):
        cols = slice(h * DH, (h + 1) * DH)
        pq = phi(q_ref[:, cols])
        parts = halves(pq)
        scores = dot3(parts, halves(phi(k_ref[:, cols])), ((1,), (1,)))
        scores = jnp.where(causal, scores, 0.0)
        phiq[h] = pq
        qh[h], ql[h] = parts
        numl[h] = dot3(halves(scores), halves(v_ref[:, cols]), ((1,), (0,)))
        denl[h] = jnp.broadcast_to(jnp.sum(scores, axis=1, keepdims=True), (tok, DH))

    z_round(3)

    def wait1(k, carry):
        origin = lax.rem(z + nz - k, nz)
        rc(ps.at[0], r1.at[origin], p1_s.at[k], p1_r.at[k], at(y, origin, c)).wait_recv()
        rc(pt, rt1.at[origin], pt_s.at[k], pt_r.at[k], at(y, origin, c)).wait_recv()
        return carry

    lax.fori_loop(1, nz, wait1, 0)
    acc = jnp.zeros((rows, DH), F32)
    acct = jnp.zeros((2, DH), F32)
    mine = jnp.zeros((2, DH), F32)
    for i in range(nz):
        s2[i] = acc
        acc = acc + r1[i]
        mine = mine + jnp.where(i < z, rt1[i], 0.0)
        acct = acct + rt1[i]
    yt[0:rows, :] = acc
    yt[rows:rows + 2, :] = acct
    yt[rows + 2:rows + 8, :] = jnp.zeros((6, DH), F32)
    for k in range(1, NY):
        go(rc(yt, yr.at[y], yx_s.at[k], yx_r.at[k], at(dy(k), z, c)))
    z_round(4)
    for k in range(1, NY):
        rc(yt, yr.at[dy(-k)], yx_s.at[k], yx_r.at[k], at(dy(k), z, c)).wait_recv()
    base = jnp.zeros((rows + 8, DH), F32)
    for yy in range(NY):
        base = base + jnp.where(yy < y, yr[yy], 0.0)
    for i in range(nz):
        s2[i] = s2[i] + base[0:rows]

    def send2(k, carry):
        peer = lax.rem(z + k, nz)
        rc(s2.at[peer], r2.at[z], p2_s.at[k], p2_r.at[k], at(y, peer, c)).start()
        return carry

    lax.fori_loop(1, nz, send2, 0)
    r2[z] = s2[z]

    mine = mine + base[rows:rows + 2]
    ft[...] = jnp.zeros_like(ft)
    ft[0:2, :] = mine + jnp.where(c == 0, tst[c, 0:2], 0.0)
    go(rc(ft, ftot.at[c], e_s.at[2], e_r.at[2], sib))
    ftot[c, 0:2, :] = mine + jnp.where(c == 1, tsx[0:2], 0.0)
    z_round(5)
    rc(ft, ftot.at[1 - c], e_s.at[2], e_r.at[2], sib).wait_recv()
    for h in range(4):
        total = ftot[h // 2, h % 2:h % 2 + 1, :]
        denl[h] = denl[h] + jnp.sum(phiq[h] * total, axis=1, keepdims=True)

    z_round(6)
    y_stage(0)
    z_round(7)
    y_stage(1)
    y_stage(2)
    z_round(8)
    y_stage(3)

    def wait2(k, carry):
        origin = lax.rem(z + nz - k, nz)
        rc(s2.at[0], r2.at[origin], p2_s.at[k], p2_r.at[k], at(y, origin, c)).wait_recv()
        return carry

    lax.fori_loop(1, nz, wait2, 0)
    fs[...] = r2[...] + jnp.where(c == 0, st[c], 0.0)
    go(rc(fs, full.at[c], e_s.at[3], e_r.at[3], sib))
    full[c] = r2[...] + jnp.where(c == 1, sx[...], 0.0)

    for t in range(4):
        h, hh = lax.rem(2 * c + t, 4), t % 2
        b = c if t < 2 else 1 - c
        if t == 2:
            rc(fs, full.at[1 - c], e_s.at[3], e_r.at[3], sib).wait_recv()
        prior = halves(full[b, hh * per:(hh + 1) * per].reshape(DH, DH))
        num = numl[h] + dot3((qh[h], ql[h]), prior, ((1,), (0,)))
        att[x, h] = num / denl[h]
        go(rc(att.at[x, h], att.at[x, h], xr_s.at[t], xr_r.at[t], right))
        go(rc(att.at[x, h], att.at[x, h], xl_s.at[t], xl_r.at[t], left))

    y_stage(4)
    y_stage(5)
    y_stage(6)
    xl, xr, xf = lax.rem(x + nx - 1, nx), lax.rem(x + 1, nx), lax.rem(x + 2, nx)
    for t in range(4):
        h = lax.rem(2 * c + t, 4)
        ref = att.at[xl, h]
        rc(ref, ref, xr_s.at[t], xr_r.at[t], right).wait_recv()
        if t % 2 == 0:
            go(rc(ref, ref, gr_s.at[t], gr_r.at[t], right))
        ref = att.at[xr, h]
        rc(ref, ref, xl_s.at[t], xl_r.at[t], left).wait_recv()
        if t % 2 == 1:
            go(rc(ref, ref, gl_s.at[t], gl_r.at[t], left))

    for r in range(7, half + 1):
        y_stage(r)
    for m in range(nz):
        far_stage(m)
    for t in range(4):
        h = lax.rem(2 * c + t, 4)
        ref = att.at[xf, h]
        if t % 2 == 0:
            rc(ref, ref, gr_s.at[t], gr_r.at[t], right).wait_recv()
        else:
            rc(ref, ref, gl_s.at[t], gl_r.at[t], left).wait_recv()
    for k in range(NY):
        for m in range(nz):
            ref = slot(dy(-k), m, 1 - c)
            rc(ref, ref, sb_s.at[k, m], sb_r.at[k, m], sib).wait_recv()

    for xx in range(nx):
        for h in range(4):
            high, low = halves(att[xx, h])
            acat[xx, 0:tok, h * DH:(h + 1) * DH] = high
            acat[xx, tok:2 * tok, h * DH:(h + 1) * DH] = low

    def tile(n, carry):
        cols = pl.ds(pl.multiple_of(n * TILE, TILE), TILE)
        total = jnp.zeros((tok, TILE), F32)
        for xx in range(nx):
            wt = w_all[xx, :, :, :, cols].reshape(4 * DH, TILE)
            high, low = halves(wt)
            both = jnp.dot(acat[xx], high, preferred_element_type=F32)
            total = total + (
                both[0:tok] + both[tok:2 * tok]
                + jnp.dot(acat[xx, 0:tok, :], low, preferred_element_type=F32)
            )
        out_ref[:, cols] = total
        return carry

    lax.fori_loop(0, out_ref.shape[1] // TILE, tile, 0)

    for copy in sends:
        copy.wait_send()

    def sent(k, carry):
        peer = lax.rem(z + k, nz)
        dev = at(y, peer, c)
        rc(ps.at[peer], r1.at[z], p1_s.at[k], p1_r.at[k], dev).wait_send()
        rc(pt, rt1.at[z], pt_s.at[k], pt_r.at[k], dev).wait_send()
        rc(s2.at[peer], r2.at[z], p2_s.at[k], p2_r.at[k], dev).wait_send()
        return carry

    lax.fori_loop(1, nz, sent, 0)


def solution(mesh):
    nz, nx = mesh.shape["seq"] // (2 * NY), mesh.shape["tp"]

    def shards(queries, keys, values, out_weight):
        tok = queries.shape[0]
        depth, columns = out_weight.shape
        part = (nz, 2 * DH // nz, DH)
        dma = pltpu.SemaphoreType.DMA
        vmem = pl.BlockSpec(memory_space=pltpu.VMEM)
        return pl.pallas_call(
            functools.partial(kernel, nz, nx),
            out_shape=jax.ShapeDtypeStruct((tok, columns), F32),
            in_specs=[pl.BlockSpec(memory_space=pltpu.HBM)] * 4,
            out_specs=vmem,
            scratch_shapes=[
                pltpu.VMEM((NY, nz, 2, depth, columns), F32),
                pltpu.VMEM((tok, 4 * DH), F32),
                pltpu.VMEM((tok, 4 * DH), F32),
                pltpu.VMEM((tok, 4 * DH), F32),
                pltpu.VMEM((2,) + part, F32),
                pltpu.VMEM((2, 8, DH), F32),
                pltpu.VMEM(part, F32),
                pltpu.VMEM((8, DH), F32),
                pltpu.VMEM(part, F32),
                pltpu.VMEM((2, DH), F32),
                pltpu.VMEM(part, F32),
                pltpu.VMEM((nz, 2, DH), F32),
                pltpu.VMEM((part[1] + 8, DH), F32),
                pltpu.VMEM((NY, part[1] + 8, DH), F32),
                pltpu.VMEM(part, F32),
                pltpu.VMEM(part, F32),
                pltpu.VMEM(part, F32),
                pltpu.VMEM((2,) + part, F32),
                pltpu.VMEM((8, DH), F32),
                pltpu.VMEM((2, 8, DH), F32),
                pltpu.VMEM((4, tok, DH), F32),
                pltpu.VMEM((4, tok, DH), BF16),
                pltpu.VMEM((4, tok, DH), BF16),
                pltpu.VMEM((4, tok, DH), F32),
                pltpu.VMEM((4, tok, DH), F32),
                pltpu.VMEM((nx, 4, tok, DH), F32),
                pltpu.VMEM((nx, 2 * tok, 4 * DH), BF16),
                dma((4,)),
                pltpu.SemaphoreType.REGULAR((nz // 2 + 1,)),
                pltpu.SemaphoreType.REGULAR((nz // 2 + 1,)),
            ]
            + [dma((nz // 2,))] * 4
            + [dma((nz,))] * 6
            + [dma((NY, nz))] * 2
            + [dma((4,))] * 2
            + [dma((nz,))] * 4
            + [dma((NY,))] * 2
            + [dma((nz,))] * 2
            + [dma((4,))] * 8,
            compiler_params=pltpu.CompilerParams(
                collective_id=0, has_side_effects=True, vmem_limit_bytes=67043328
            ),
        )(queries, keys, values, out_weight)

    return jax.shard_map(
        shards,
        mesh=mesh,
        in_specs=(P("seq", "tp"),) * 4,
        out_specs=P("seq", "tp"),
        check_vma=False,
    )
```

time: 77.4 us -> 75.2 us (0.972)
  local copies, waits for them, and re-layouts: 4.48 us -> 1.89 us
    unnamed x9 -> x1, local copies, waits for them, and re-layouts: 4.48 us -> 1.89 us
where the time goes in v2:
time: 75.2 us; the launch traced here: 75 us
  Pallas kernels  73.1 us (97%)
  local copies, waits for them, and re-layouts  1.89 us (3%)
    pallas_call x1, Pallas kernels, shards(): pl.pallas_call(functools.partial(kernel, nz, nx), out_shape=jax.ShapeDtyp...  73.1 us
    unnamed x1, local copies, waits for them, and re-layouts  1.89 us

profile of v2, /device:TPU:1, one launch (start us, length us, event | category | flops | bytes accessed | tf_op | source)
XLA Modules:
  0.0 75.0 jit_solution(5862027319855743749)
XLA Ops:
  0.0 73.1 %shard_map.46 = f32[128,1024]{1,0:T(8,128)} custom-call(f32[128,512]{1,0:T(8,128)} %q_hbm.1, f32[128,512]{1,0:T(8,128)} %k_hbm.1, f32[128,512]{1,0:T(8,128)} %v_hbm.1, f32[16,1024]{1,0:T(8,128)} %w_hbm.1), custom_call_target="tpu_custom_call" | custom-call | tf_op jit(solution)/shard_map/pallas_call | solution.py:370
  73.1 1.9 %copy.6 = f32[128,1024]{1,0:T(8,128)} copy(f32[128,1024]{1,0:T(8,128)} %shard_map.46) | data formatting | bytes 1048576

commit v3 on v2

--- a/solution.py
+++ b/solution.py
@@ -68,10 +68,11 @@
     sib = at(y, z, 1 - c)
     right, left = {"tp": lax.rem(x + 1, nx)}, {"tp": lax.rem(x + nx - 1, nx)}
     up, down = at(y, dz(1), c), at(y, dz(-1), c)
+    up2, down2 = at(y, dz(2), c), at(y, dz(-2), c)
     half = nz // 2
 
     barrier = pltpu.get_barrier_semaphore()
-    near = [sib, right, left, up, down] + [at(dy(k), z, c) for k in range(1, NY)]
+    near = [sib, right, left, up, down, up2, down2] + [at(dy(k), z, c) for k in range(1, NY)]
     for dev in near:
         pl.semaphore_signal(barrier, inc=1, device_id=dev, device_id_type=MESH)
     inputs = [
@@ -84,16 +85,13 @@
         copy.start()
     pl.semaphore_wait(barrier, len(near))
 
-    def token(r):
-        if r > 1:
-            pl.semaphore_wait(tok_l.at[r], 1)
-        if r < half:
-            pl.semaphore_signal(tok_l.at[r + 1], inc=1, device_id=down, device_id_type=MESH)
-        if r < half:
-            if r > 1:
-                pl.semaphore_wait(tok_r.at[r], 1)
-            if r < half - 1:
-                pl.semaphore_signal(tok_r.at[r + 1], inc=1, device_id=up, device_id_type=MESH)
+    def token(j):
+        if j > 1:
+            pl.semaphore_wait(tok_l.at[j - 1], 1)
+            pl.semaphore_wait(tok_r.at[j - 1], 1)
+        if 2 * j < half:
+            pl.semaphore_signal(tok_l.at[j], inc=1, device_id=down2, device_id_type=MESH)
+            pl.semaphore_signal(tok_r.at[j], inc=1, device_id=up2, device_id_type=MESH)
 
     sends = []
 
@@ -117,25 +115,56 @@
         go(rc(src, dst, ym_s.at[m], ym_r.at[m], at(dy(-1), z, c)))
         go(rc(src, dst, sb_s.at[0, m], sb_r.at[0, m], sib))
 
+    def pass_on(m, d):
+        ref = slot(y, m, c)
+        if m <= half:
+            if d + 2 <= half:
+                go(rc(ref, ref, zr_s.at[d + 1], zr_r.at[d + 1], up2))
+            if d + 1 <= half:
+                go(rc(ref, ref, zr_s.at[d], zr_r.at[d], up))
+        else:
+            if d + 2 < half:
+                go(rc(ref, ref, zl_s.at[d + 1], zl_r.at[d + 1], down2))
+            if d + 1 < half:
+                go(rc(ref, ref, zl_s.at[d], zl_r.at[d], down))
+
     def z_round(r):
         if r == 0:
-            dst = slot(y, 0, c)
-            go(rc(dst, dst, zr_s.at[0], zr_r.at[0], at(y, dz(1), c)))
-            go(rc(dst, dst, zl_s.at[0], zl_r.at[0], at(y, dz(-1), c)))
+            ref = slot(y, 0, c)
+            go(rc(ref, ref, zr_s.at[1], zr_r.at[1], up2))
+            go(rc(ref, ref, zl_s.at[1], zl_r.at[1], down2))
+            go(rc(ref, ref, zr_s.at[0], zr_r.at[0], up))
+            go(rc(ref, ref, zl_s.at[0], zl_r.at[0], down))
             have(0)
             return
-        ref = slot(y, r, c)
-        rc(ref, ref, zr_s.at[r - 1], zr_r.at[r - 1], at(y, dz(1), c)).wait_recv()
-        if r < half:
-            go(rc(ref, ref, zr_s.at[r], zr_r.at[r], at(y, dz(1), c)))
-        if r < half:
-            ref = slot(y, half + r, c)
-            rc(ref, ref, zl_s.at[r - 1], zl_r.at[r - 1], at(y, dz(-1), c)).wait_recv()
-            if r < half - 1:
-                go(rc(ref, ref, zl_s.at[r], zl_r.at[r], at(y, dz(-1), c)))
-        have(r)
-        if r < half:
-            have(half + r)
+        for d in (2 * r, 2 * r - 1):
+            ref = slot(y, d, c)
+            rc(ref, ref, zr_s.at[d - 1], zr_r.at[d - 1], up).wait_recv()
+            if d == 2 * r:
+                pass_on(d, d)
+            if d < half:
+                ref = slot(y, half + d, c)
+                rc(ref, ref, zl_s.at[d - 1], zl_r.at[d - 1], down).wait_recv()
+                if d == 2 * r:
+                    pass_on(half + d, d)
+        if r not in (3,):
+            spread(r)
+
+    def spread(r):
+        for d in (2 * r - 1, 2 * r):
+            have(d)
+            if d < half:
+                have(half + d)
+
+    late = []
+
+    def push(k, m):
+        late.append((k, m))
+
+    def flush():
+        for k, m in late:
+            to_sib(k, m)
+        late.clear()
 
     def y_stage(r):
         for m in ((r,) if r in (0, half) else (r, half + r)):
@@ -143,11 +172,11 @@
             rc(below, below, yp_s.at[m], yp_r.at[m], at(dy(1), z, c)).wait_recv()
             if m < half:
                 go(rc(below, below, fd_s.at[m], fd_r.at[m], at(dy(1), z, c)))
-            to_sib(1, m)
+            push(1, m)
             rc(above, above, ym_s.at[m], ym_r.at[m], at(dy(-1), z, c)).wait_recv()
             if m >= half:
                 go(rc(above, above, fd_s.at[m], fd_r.at[m], at(dy(-1), z, c)))
-            to_sib(3, m)
+            push(3, m)
 
     def far_stage(m):
         ref = slot(dy(2), m, c)
@@ -161,7 +190,7 @@
     inputs[2].wait()
     row8 = lax.broadcasted_iota(jnp.int32, (8, DH), 0)
     per = nz // 2
-    hops = ((2, 3), (4, 5), (6,), (7, 8))
+    hops = ((2,), (3,), (4,), ())
     for t in range(4):
         b, hh = (1 - c if t < 2 else c), t % 2
         cols = pl.ds(pl.multiple_of((2 * b + hh) * DH, DH), DH)
@@ -178,7 +207,7 @@
             go(rc(tst.at[b], tsx, e_s.at[1], e_r.at[1], sib))
         for r in hops[t]:
             token(r)
-        if t == 2:
+        if t == 1:
             z_round(1)
     rc(st.at[1 - c], sx, e_s.at[0], e_r.at[0], sib).wait_recv()
     rc(tst.at[1 - c], tsx, e_s.at[1], e_r.at[1], sib).wait_recv()
@@ -195,7 +224,6 @@
     r1[z] = ps[z]
     rt1[z] = pt[...]
     yr[y] = jnp.zeros((rows + 8, DH), F32)
-    z_round(2)
 
     inputs[3].wait()
     causal = lax.broadcasted_iota(jnp.int32, (tok, tok), 0) >= lax.broadcasted_iota(
@@ -211,8 +239,8 @@
         qh[h], ql[h] = parts
         numl[h] = dot3(halves(scores), halves(v_ref[:, cols]), ((1,), (0,)))
         denl[h] = jnp.broadcast_to(jnp.sum(scores, axis=1, keepdims=True), (tok, DH))
-
-    z_round(3)
+        if h == 1:
+            z_round(2)
 
     def wait1(k, carry):
         origin = lax.rem(z + nz - k, nz)
@@ -234,7 +262,9 @@
     yt[rows + 2:rows + 8, :] = jnp.zeros((6, DH), F32)
     for k in range(1, NY):
         go(rc(yt, yr.at[y], yx_s.at[k], yx_r.at[k], at(dy(k), z, c)))
-    z_round(4)
+    z_round(3)
+    spread(3)
+    y_stage(0)
     for k in range(1, NY):
         rc(yt, yr.at[dy(-k)], yx_s.at[k], yx_r.at[k], at(dy(k), z, c)).wait_recv()
     base = jnp.zeros((rows + 8, DH), F32)
@@ -256,19 +286,14 @@
     ft[0:2, :] = mine + jnp.where(c == 0, tst[c, 0:2], 0.0)
     go(rc(ft, ftot.at[c], e_s.at[2], e_r.at[2], sib))
     ftot[c, 0:2, :] = mine + jnp.where(c == 1, tsx[0:2], 0.0)
-    z_round(5)
+    z_round(4)
     rc(ft, ftot.at[1 - c], e_s.at[2], e_r.at[2], sib).wait_recv()
     for h in range(4):
         total = ftot[h // 2, h % 2:h % 2 + 1, :]
         denl[h] = denl[h] + jnp.sum(phiq[h] * total, axis=1, keepdims=True)
 
-    z_round(6)
-    y_stage(0)
-    z_round(7)
-    y_stage(1)
-    y_stage(2)
-    z_round(8)
-    y_stage(3)
+    for r in range(1, 5):
+        y_stage(r)
 
     def wait2(k, carry):
         origin = lax.rem(z + nz - k, nz)
@@ -291,9 +316,10 @@
         go(rc(att.at[x, h], att.at[x, h], xr_s.at[t], xr_r.at[t], right))
         go(rc(att.at[x, h], att.at[x, h], xl_s.at[t], xl_r.at[t], left))
 
-    y_stage(4)
+    flush()
     y_stage(5)
     y_stage(6)
+    flush()
     xl, xr, xf = lax.rem(x + nx - 1, nx), lax.rem(x + 1, nx), lax.rem(x + 2, nx)
     for t in range(4):
         h = lax.rem(2 * c + t, 4)
@@ -305,9 +331,10 @@
         rc(ref, ref, xl_s.at[t], xl_r.at[t], left).wait_recv()
         if t % 2 == 1:
             go(rc(ref, ref, gl_s.at[t], gl_r.at[t], left))
-
-    for r in range(7, half + 1):
-        y_stage(r)
+        if t % 2 == 1:
+            y_stage(7 + t // 2)
+            flush()
+
     for m in range(nz):
         far_stage(m)
     for t in range(4):

time: 75.2 us -> 70 us (0.931)
  Pallas kernels: 73.1 us -> 68 us
    pallas_call x1, Pallas kernels: 73.1 us -> 68 us  [shards(): pl.pallas_call(functools.partial(kernel, nz, nx), out_shape=jax.ShapeDtyp...]
where the time goes in v3:
time: 70 us; the launch traced here: 69.9 us
  Pallas kernels  68 us (97%)
  local copies, waits for them, and re-layouts  1.89 us (3%)
    pallas_call x1, Pallas kernels, shards(): pl.pallas_call(functools.partial(kernel, nz, nx), out_shape=jax.ShapeDtyp...  68 us
    unnamed x1, local copies, waits for them, and re-layouts  1.89 us

profile of v3, /device:TPU:1, one launch (start us, length us, event | category | flops | bytes accessed | tf_op | source)
XLA Modules:
  0.0 69.9 jit_solution(9574097641605792873)
XLA Ops:
  0.0 68.0 %shard_map.46 = f32[128,1024]{1,0:T(8,128)} custom-call(f32[128,512]{1,0:T(8,128)} %q_hbm.1, f32[128,512]{1,0:T(8,128)} %k_hbm.1, f32[128,512]{1,0:T(8,128)} %v_hbm.1, f32[16,1024]{1,0:T(8,128)} %w_hbm.1), custom_call_target="tpu_custom_call" | custom-call | tf_op jit(solution)/shard_map/pallas_call | solution.py:397
  68.0 1.9 %copy.6 = f32[128,1024]{1,0:T(8,128)} copy(f32[128,1024]{1,0:T(8,128)} %shard_map.46) | data formatting | bytes 1048576

commit v4 on v3

--- a/solution.py
+++ b/solution.py
@@ -239,8 +239,8 @@
         qh[h], ql[h] = parts
         numl[h] = dot3(halves(scores), halves(v_ref[:, cols]), ((1,), (0,)))
         denl[h] = jnp.broadcast_to(jnp.sum(scores, axis=1, keepdims=True), (tok, DH))
-        if h == 1:
-            z_round(2)
+
+    z_round(2)
 
     def wait1(k, carry):
         origin = lax.rem(z + nz - k, nz)
@@ -335,7 +335,7 @@
             y_stage(7 + t // 2)
             flush()
 
-    for m in range(nz):
+    for m in [0] + [m for r in range(1, half) for m in (half + r, r)] + [half]:
         far_stage(m)
     for t in range(4):
         h = lax.rem(2 * c + t, 4)

time: 70 us -> 69.4 us (level)
  Pallas kernels: 68 us -> 67.3 us
where the time goes in v4:
time: 69.4 us; the launch traced here: 69.2 us
  Pallas kernels  67.3 us (97%)
  local copies, waits for them, and re-layouts  1.89 us (3%)
    pallas_call x1, Pallas kernels, shards(): pl.pallas_call(functools.partial(kernel, nz, nx), out_shape=jax.ShapeDtyp...  67.3 us
    unnamed x1, local copies, waits for them, and re-layouts  1.89 us

profile of v4, /device:TPU:1, one launch (start us, length us, event | category | flops | bytes accessed | tf_op | source)
XLA Modules:
  0.0 69.2 jit_solution(12161118916897184542)
XLA Ops:
  0.0 67.3 %shard_map.46 = f32[128,1024]{1,0:T(8,128)} custom-call(f32[128,512]{1,0:T(8,128)} %q_hbm.1, f32[128,512]{1,0:T(8,128)} %k_hbm.1, f32[128,512]{1,0:T(8,128)} %v_hbm.1, f32[16,1024]{1,0:T(8,128)} %w_hbm.1), custom_call_target="tpu_custom_call" | custom-call | tf_op jit(solution)/shard_map/pallas_call | solution.py:397
  67.3 1.9 %copy.6 = f32[128,1024]{1,0:T(8,128)} copy(f32[128,1024]{1,0:T(8,128)} %shard_map.46) | data formatting | bytes 1048576
